TPU v7x, 32 devices: a whole 2x2x4 slice. The times are simulated.
32 devices in a mesh: ia: 4 (over z), ja: 4 (over x, core), ka: 2 (over y).
Axes of the slice: x: 2, y: 2, z: 4, core: 2. Of those that a mesh axis runs over, the one named last changes fastest.
Arguments:
- tensor: bfloat16 [64, 256, 512], P('ka', 'ia', 'ja'), may hold values from -768 to 768
- observed: int32 [64, 256, 512], P('ka', 'ia', 'ja'), may hold values from 0 to 1, as said below
- factor_a: bfloat16 [256, 128], P('ia', ('ja', 'ka')), may hold values from -6 to 6
- factor_b: bfloat16 [512, 128], P('ja', ('ia', 'ka')), may hold values from -6 to 6
- factor_c: bfloat16 [64, 128], P('ka', ('ia', 'ja')), may hold values from -6 to 6
Outputs:
- step_a: float32 [256, 128], P('ia', ('ja', 'ka'))
- step_b: float32 [512, 128], P('ja', ('ia', 'ka'))
- step_c: float32 [64, 128], P('ka', ('ia', 'ja'))
Inputs may be any that keep to these rules, and one draw needn't show every extreme that they name: `observed`: a 0/1 weight per cell.
All inputs are finite; a program needn't handle non-finite values.
Results may differ from a plain program's by a relative error of at most 0.0095.
Values may be sent and summed in bfloat16 or wider, within the bound.
A program may use at most 64 MiB of HBM per device.

v0:
```python
import jax
import jax.numpy as jnp
from jax import lax
from jax.sharding import PartitionSpec as P

ITERS = 2


DAMP = 1.0


def against(left_side, right_side):
    return lax.dot_general(
        left_side, right_side, (((1,), (1,)), ((), ())), preferred_element_type=jnp.float32
    )


def local(tensor, observed, factor_a, factor_b, factor_c):
    depth_rows, height_rows, width_cols = tensor.shape
    divisor = width_cols * lax.axis_size("ja") * (depth_rows * lax.axis_size("ka")) / 32.0
    full_a = lax.all_gather(factor_a, ("ja", "ka"), axis=1, tiled=True)
    full_b = lax.all_gather(factor_b, ("ia", "ka"), axis=1, tiled=True)
    full_c = lax.all_gather(factor_c, ("ia", "ja"), axis=1, tiled=True)
    columns = full_a.shape[1]
    wide_a = full_a.astype(jnp.float32)
    wide_c = full_c.astype(jnp.float32)
    weight = (observed.astype(jnp.float32) * (1.0 / divisor)).astype(jnp.bfloat16)
    weight = weight.reshape(depth_rows * height_rows, width_cols)
    paired = (
        (wide_c[:, None, :] * wide_a[None, :, :])
        .astype(jnp.bfloat16)
        .reshape(depth_rows * height_rows, columns)
    )

    def partials(weighted):
        part_b = lax.dot_general(
            weighted, paired, (((0,), (0,)), ((), ())), preferred_element_type=jnp.float32
        )
        mixture = jnp.dot(weighted, full_b, preferred_element_type=jnp.float32).reshape(
            depth_rows, height_rows, columns
        )
        part_a = jnp.einsum("kir,kr->ir", mixture, wide_c)
        part_c = jnp.einsum("kir,ir->kr", mixture, wide_a)
        return (part_a, part_b, part_c)

    def settle(parts):
        total_a = lax.psum(parts[0], ("ja", "ka"))
        total_b = lax.psum(parts[1], ("ia", "ka"))
        total_c = lax.psum(parts[2], ("ia", "ja"))
        return (total_a, total_b, total_c)

    scales = (
        1.0 / lax.axis_size(("ja", "ka")),
        1.0 / lax.axis_size(("ia", "ka")),
        1.0 / lax.axis_size(("ia", "ja")),
    )

    def inner_sum(first, second):
        local_sum = sum(
            (
                jnp.sum(left_side * right_side) * factor
                for left_side, right_side, factor in zip(first, second, scales)
            )
        )
        return lax.psum(local_sum, ("ia", "ja", "ka"))

    def expand(direction):
        hat_a = direction[0].astype(jnp.bfloat16)
        hat_b = direction[1].astype(jnp.bfloat16)
        hat_c = direction[2].astype(jnp.bfloat16)
        return (hat_a, hat_b, hat_c)

    def hessian_times(direction):
        hat_a, hat_b, hat_c = expand(direction)
        sideways = (
            hat_c.astype(jnp.float32)[:, None, :] * wide_a[None, :, :]
            + wide_c[:, None, :] * hat_a.astype(jnp.float32)[None, :, :]
        )
        sideways = sideways.astype(jnp.bfloat16).reshape(depth_rows * height_rows, columns)
        tangent = against(paired, hat_b) + against(sideways, full_b)
        weighted = (weight.astype(jnp.float32) * tangent).astype(jnp.bfloat16)
        parts = settle(partials(weighted))
        return tuple((part + DAMP * vector for part, vector in zip(parts, direction)))

    fitted = against(paired, full_b)
    values = tensor.reshape(depth_rows * height_rows, width_cols).astype(jnp.float32)
    errors = (weight.astype(jnp.float32) * (values - fitted)).astype(jnp.bfloat16)
    gradient = settle(partials(errors))
    solution = tuple((jnp.zeros_like(vector) for vector in gradient))
    residual = gradient
    direction = gradient
    norm_now = inner_sum(residual, residual)
    for iteration in range(ITERS):
        product = hessian_times(direction)
        step_size = norm_now / inner_sum(direction, product)
        solution = tuple(
            (vector + step_size * update for vector, update in zip(solution, direction))
        )
        if iteration + 1 < ITERS:
            residual = tuple(
                (vector - step_size * update for vector, update in zip(residual, product))
            )
            norm_next = inner_sum(residual, residual)
            direction = tuple(
                (
                    vector + norm_next / norm_now * update
                    for vector, update in zip(residual, direction)
                )
            )
            norm_now = norm_next
    position_a = lax.axis_index(("ja", "ka")) * factor_a.shape[1]
    position_b = lax.axis_index(("ia", "ka")) * factor_b.shape[1]
    position_c = lax.axis_index(("ia", "ja")) * factor_c.shape[1]
    step_a = lax.dynamic_slice_in_dim(solution[0], position_a, factor_a.shape[1], 1)
    step_b = lax.dynamic_slice_in_dim(solution[1], position_b, factor_b.shape[1], 1)
    step_c = lax.dynamic_slice_in_dim(solution[2], position_c, factor_c.shape[1], 1)
    return (step_a, step_b, step_c)


def solution(mesh):
    placed = (
        P("ka", "ia", "ja"),
        P("ka", "ia", "ja"),
        P("ia", ("ja", "ka")),
        P("ja", ("ia", "ka")),
        P("ka", ("ia", "ja")),
    )
    return jax.shard_map(
        local,
        mesh=mesh,
        in_specs=placed,
        out_specs=(P("ia", ("ja", "ka")), P("ja", ("ia", "ka")), P("ka", ("ia", "ja"))),
        check_vma=False,
    )
```

profile of v0, /device:TPU:0, one launch (start us, length us, event | category | flops | bytes accessed | tf_op | source)
XLA Modules:
  0.0 519.4 jit_solution(12304898515846047202)
XLA Ops:
  7.2 14.5 %all_gather.10 = bf16[64,128]{0,1:T(8,128)(2,1)S(1)} all-gather(bf16[64,16]{0,1:T(8,128)(2,1)} %param.7), channel_id=1, replica_groups=mesh['ia'=4,'ja'=4,'ka'=2] {'ja','ka'}, dimensions={1}, use_global_device_ids=true | all-gather | bytes 18432 | tf_op jit(solution)/shard_map/all_gather | solution.py:21
  21.8 0.7 copy-done.3
  22.4 21.9 %all_gather.9 = bf16[32,128]{0,1:T(8,128)(2,1)S(1)} all-gather(bf16[32,8]{0,1:T(8,128)(2,1)S(1)} %copy-done.3), channel_id=1, replica_groups=mesh['ia'=4,'ja'=4,'ka'=2] {'ia','ja'}, dimensions={1}, use_global_device_ids=true | all-gather | bytes 8704 | tf_op jit(solution)/shard_map/all_gather | solution.py:23
  44.4 0.7 copy-done.2
  45.1 30.6 %all_gather.11 = bf16[128,128]{0,1:T(8,128)(2,1)S(1)} all-gather(bf16[128,16]{0,1:T(8,128)(2,1)S(1)} %copy-done.2), channel_id=1, replica_groups=mesh['ia'=4,'ja'=4,'ka'=2] {'ia','ka'}, dimensions={1}, use_global_device_ids=true | all-gather | bytes 36864 | tf_op jit(solution)/shard_map/all_gather | solution.py:22
  75.7 1.4 multiply_convert_fusion.1
  77.2 0.9 copy-done.1
  78.4 1.0 fusion.16
  80.1 22.7 %psum.91 = f32[64,128]{1,0:T(8,128)S(1)} all-reduce(f32[64,128]{1,0:T(8,128)S(1)} %bitcast.75), channel_id=1, replica_groups=mesh['ia'=4,'ja'=4,'ka'=2] {'ja','ka'}, use_global_device_ids=true, to_apply=%region_0.0 | all-reduce | flops 8192 | bytes 65536 | tf_op jit(solution)/shard_map/psum | solution.py:47
  102.8 58.1 %psum.93 = f32[32,128]{1,0:T(8,128)S(1)} all-reduce(f32[32,128]{1,0:T(8,128)S(1)} %bitcast.78), channel_id=1, replica_groups=mesh['ia'=4,'ja'=4,'ka'=2] {'ia','ja'}, use_global_device_ids=true, to_apply=%region_4.0 | all-reduce | flops 4096 | bytes 32768 | tf_op jit(solution)/shard_map/psum | solution.py:49
  161.0 1.1 fusion.12
  162.5 1.0 fusion.17
  164.0 23.9 %psum.95 = f32[64,128]{1,0:T(8,128)S(1)} all-reduce(f32[64,128]{1,0:T(8,128)S(1)} %bitcast.76), channel_id=1, replica_groups=mesh['ia'=4,'ja'=4,'ka'=2] {'ja','ka'}, use_global_device_ids=true, to_apply=%region_7.0 | all-reduce | flops 8192 | bytes 65536 | tf_op jit(solution)/shard_map/psum | solution.py:47
  187.8 0.6 multiply_reduce_fusion.10
  188.4 57.7 %psum.97 = f32[32,128]{1,0:T(8,128)S(1)} all-reduce(f32[32,128]{1,0:T(8,128)S(1)} %bitcast.77), channel_id=1, replica_groups=mesh['ia'=4,'ja'=4,'ka'=2] {'ia','ja'}, use_global_device_ids=true, to_apply=%region_11.0 | all-reduce | flops 4096 | bytes 32768 | tf_op jit(solution)/shard_map/psum | solution.py:49
  246.2 0.7 multiply_reduce_fusion.13
  248.1 1.5 multiply_reduce_fusion.7
  252.3 36.9 %all-reduce = (f32[]{:T(128)}, f32[]{:T(128)}) all-reduce(f32[]{:T(128)S(6)} %add.125, f32[]{:T(128)S(6)} %add.132), channel_id=1, replica_groups=mesh['ia'=4,'ja'=4,'ka'=2] {'ia','ja','ka'}, use_global_device_ids=true, to_apply=%region_6.0 | all-reduce | flops 2 | bytes 16 | tf_op jit(solution)/shard_map/psum | solution.py:65
  290.5 0.6 multiply_reduce_fusion.12
  291.8 0.6 multiply_reduce_fusion.9
  292.4 0.6 multiply_reduce_fusion.6
  294.3 41.9 %psum.99 = f32[]{:T(128)} all-reduce(f32[]{:T(128)S(6)} %add.134), channel_id=1, replica_groups=mesh['ia'=4,'ja'=4,'ka'=2] {'ia','ja','ka'}, use_global_device_ids=true, to_apply=%region_17.0 | all-reduce | flops 1 | bytes 8 | tf_op jit(solution)/shard_map/psum | solution.py:65
  338.7 1.0 fusion.18
  339.6 59.3 %psum.102 = f32[32,128]{1,0:T(8,128)S(1)} all-reduce(f32[32,128]{1,0:T(8,128)S(1)} %bitcast.79), channel_id=1, replica_groups=mesh['ia'=4,'ja'=4,'ka'=2] {'ia','ja'}, use_global_device_ids=true, to_apply=%region_22.0 | all-reduce | flops 4096 | bytes 32768 | tf_op jit(solution)/shard_map/psum | solution.py:49
  400.3 23.2 %psum.100 = f32[64,128]{1,0:T(8,128)S(1)} all-reduce(f32[64,128]{1,0:T(8,128)S(1)} %bitcast.74), channel_id=1, replica_groups=mesh['ia'=4,'ja'=4,'ka'=2] {'ja','ka'}, use_global_device_ids=true, to_apply=%region_18.0 | all-reduce | flops 8192 | bytes 65536 | tf_op jit(solution)/shard_map/psum | solution.py:47
  423.5 0.6 fusion.8
  424.1 42.1 %all-reduce.9.cloned.1.call-done = f32[128,128]{1,0:T(8,128)} async-done(((f32[128,128]{1,0:T(8,128)}), f32[128,128]{1,0:T(8,128)}) %all-reduce.9.cloned.1.call-update) | async-done | bytes 65552 | tf_op jit(solution)/shard_map/psum | solution.py:48
  466.2 1.5 fusion.6
  469.0 40.3 %psum.103 = f32[]{:T(128)} all-reduce(f32[]{:T(128)S(6)} %add.144), channel_id=1, replica_groups=mesh['ia'=4,'ja'=4,'ka'=2] {'ia','ja','ka'}, use_global_device_ids=true, to_apply=%region_24.0 | all-reduce | flops 1 | bytes 8 | tf_op jit(solution)/shard_map/psum | solution.py:65
  510.7 0.7 copy.24
  511.5 0.7 copy.23
  512.2 0.7 copy.22
  (43 shorter events, 4.4 us)
Async XLA Ops:
  7.2 153.9 %all-reduce.5.cloned.1.call-start = ((), (), s32[]{:S(2)}) async-start(), calls=%async_computation | async-start | bytes 131072 | tf_op jit(solution)/shard_map/psum | solution.py:48
  21.8 0.7 copy-start.3
  44.4 0.7 copy-start.2
  77.0 1.0 copy-start.1
  79.4 168.7 %all-reduce.7.cloned.1.call-start = ((), (), s32[]{:S(2)}) async-start(), calls=%async_computation.1 | async-start | bytes 131072 | tf_op jit(solution)/shard_map/psum | solution.py:48
  163.8 302.5 %all-reduce.9.cloned.1.call-start = ((), (), s32[]{:S(2)}) async-start(), calls=%async_computation.2 | async-start | bytes 131072 | tf_op jit(solution)/shard_map/psum | solution.py:48
  188.4 59.7 %copy-start = (f32[128,128]{1,0:T(8,128)S(1)}, f32[128,128]{1,0:T(8,128)}, u32[]{:S(2)}) copy-start(f32[128,128]{1,0:T(8,128)} %all-reduce.5.cloned.1.call-done) | copy-start | bytes 196612
Sparse Core Ops, SparseCore 0:
  79.5 66.1 all-reduce.4
  163.9 66.5 all-reduce.6
  400.3 65.8 all-reduce.8
where the time goes:
time: 520 us; the launch traced here: 519 us
  blocking collectives  431 us (83%)
  waiting for transfers between devices  42.2 us (8%)
  between operations  25.8 us (5%)
  other arithmetic  9.88 us (2%)
  matrix products  6.15 us (1%)
    psum x3, blocking collectives, settle(): total_c = lax.psum(parts[2], ('ia', 'ja'))  175 us
    psum x3, blocking collectives, inner_sum(): return lax.psum(local_sum, ('ia', 'ja', 'ka'))  119 us
    psum x3, blocking collectives, settle(): total_a = lax.psum(parts[0], ('ja', 'ka'))  69.7 us
    psum x3, waiting for transfers between devices, settle(): total_b = lax.psum(parts[1], ('ia', 'ka'))  42.1 us
    all_gather x1, blocking collectives, local(): full_b = lax.all_gather(factor_b, ('ia', 'ka'), axis=1, tiled=True)  30.6 us
    all_gather x1, blocking collectives, local(): full_c = lax.all_gather(factor_c, ('ia', 'ja'), axis=1, tiled=True)  21.9 us
    all_gather x1, blocking collectives, local(): full_a = lax.all_gather(factor_a, ('ja', 'ka'), axis=1, tiled=True)  14.5 us
  transfers between devices with their start and end apart: 3, of which 1 were waited for; matrix products, arithmetic and copies ran while one was open for 1% of the time, Pallas kernels for 0%

commit v1 on v0

v1 whole, which is shorter than its diff:
```python
import functools

import jax
import jax.numpy as jnp
from jax import lax
from jax.experimental import pallas as pl
from jax.experimental.pallas import tpu as pltpu
from jax.sharding import PartitionSpec as P

DAMP = 1.0
CHUNK_K = 8
UNROLL = 40
F32 = jnp.float32
BF16 = jnp.bfloat16


def each(count, body):
    if count <= UNROLL:
        for step in range(1, count):
            body(step)
    else:
        lax.fori_loop(1, count, lambda step, carry: (body(step), carry)[1], 0)


def mm(left, right):
    return jnp.dot(left, right, preferred_element_type=F32)


def total(array):
    rows, cols = array.shape
    folded = jnp.sum(array.reshape(rows // 8, 8, cols), axis=0) if rows > 8 else array
    return jnp.sum(jnp.sum(folded, axis=0, keepdims=True), axis=1, keepdims=True)


def kernel(
    sizes,
    inverse,
    tensor_hbm,
    observed_hbm,
    fa_hbm,
    fb_hbm,
    fc_hbm,
    out_a,
    out_b,
    out_c,
    tensor,
    observed,
    slot_a,
    slot_b,
    slot_c,
    flip_a,
    flip_b,
    flip_c,
    paired,
    paired_t,
    first_t,
    send_a,
    send_b,
    send_c,
    recv_a,
    recv_b,
    recv_c,
    grad_a,
    grad_b,
    grad_c,
    send_s,
    recv_s,
    load_sem,
    gather_send,
    gather_recv,
    part_send,
    part_recv,
    scal_send,
    scal_recv,
):
    size_i, size_j, size_k = sizes
    ia, ja, ka = lax.axis_index("ia"), lax.axis_index("ja"), lax.axis_index("ka")
    count_a, count_b, count_c = size_j * size_k, size_i * size_k, size_i * size_j
    count = size_i * size_j * size_k
    rank_a, rank_b, rank_c = ja * size_k + ka, ia * size_k + ka, ia * size_j + ja
    rank = rank_c * size_k + ka

    def peer_a(step):
        other = lax.rem(rank_a + step, count_a)
        return (ia, lax.div(other, size_k), lax.rem(other, size_k))

    def peer_b(step):
        other = lax.rem(rank_b + step, count_b)
        return (lax.div(other, size_k), ja, lax.rem(other, size_k))

    def peer_c(step):
        other = lax.rem(rank_c + step, count_c)
        return (lax.div(other, size_j), lax.rem(other, size_j), ka)

    def peer_all(step):
        other = lax.rem(rank + step, count)
        pair = lax.div(other, size_k)
        return (lax.div(pair, size_j), lax.rem(pair, size_j), lax.rem(other, size_k))

    groups = ((count_a, peer_a), (count_b, peer_b), (count_c, peer_c))

    def send(source, target, send_sem, recv_sem, peer):
        pltpu.make_async_remote_copy(
            src_ref=source,
            dst_ref=target,
            send_sem=send_sem,
            recv_sem=recv_sem,
            device_id=peer,
            device_id_type=pl.DeviceIdType.MESH,
        ).start()

    def await_bytes(like, sem):
        pltpu.make_async_copy(like, like, sem).wait()

    load_tensor = pltpu.make_async_copy(tensor_hbm, tensor, load_sem.at[0])
    load_observed = pltpu.make_async_copy(observed_hbm, observed, load_sem.at[1])
    shards = ((fa_hbm, slot_a, rank_a), (fb_hbm, slot_b, rank_b), (fc_hbm, slot_c, rank_c))
    for index, (shard, slots, own) in enumerate(shards):
        pltpu.make_async_copy(shard, slots.at[own], gather_recv.at[index]).start()
    load_tensor.start()
    load_observed.start()

    barrier = pltpu.get_barrier_semaphore()

    def greet(step):
        pl.semaphore_signal(
            barrier, inc=1, device_id=peer_all(step), device_id_type=pl.DeviceIdType.MESH
        )

    each(count, greet)
    pl.semaphore_wait(barrier, count - 1)

    for index in (1, 0, 2):
        shard, slots, own = shards[index]
        members, peer = groups[index]

        def gather(step):
            send(shard, slots.at[own], gather_send.at[index], gather_recv.at[index], peer(step))

        each(members, gather)

    def assemble(index, slots, flip):
        await_bytes(slots, gather_recv.at[index])
        members, width, _ = slots.shape
        for step in range(members):
            flip[step * width : (step + 1) * width, :] = slots[step].astype(F32)
        return flip[...]

    wide_a = assemble(0, slot_a, flip_a).T
    wide_c = assemble(2, slot_c, flip_c).T
    turned_b = assemble(1, slot_b, flip_b)
    bt = turned_b.astype(BF16)
    full_b = turned_b.T.astype(BF16)
    depth, height, width = tensor.shape
    columns = wide_a.shape[1]
    rows = CHUNK_K * height
    chunks = depth // CHUNK_K
    load_tensor.wait()
    load_observed.wait()

    def weight_of(chunk):
        cells = observed[chunk * CHUNK_K : (chunk + 1) * CHUNK_K].reshape(rows, width)
        return cells.astype(F32) * inverse

    def pick(wide, chunk):
        return wide[chunk * CHUNK_K : (chunk + 1) * CHUNK_K][:, None, :]

    def spread(weighted, chunk, sums):
        mixture = mm(weighted, full_b).reshape(CHUNK_K, height, columns)
        sum_a = jnp.sum(mixture * pick(wide_c, chunk), axis=0)
        sum_c = jnp.sum(mixture * wide_a[None, :, :], axis=1)
        sum_b = mm(paired_t[:, chunk * rows : (chunk + 1) * rows], weighted)
        if sums is None:
            return [sum_a, sum_b, [sum_c]]
        return [sums[0] + sum_a, sums[1] + sum_b, sums[2] + [sum_c]]

    def fold(array):
        return jnp.sum(array.reshape(rows // 8, 8, width), axis=0)

    def share(turn, sums):
        own = (sums[0], sums[1], jnp.concatenate(sums[2], axis=0))
        for index, (outbox, inbox) in ((1, (send_b, recv_b)), (0, (send_a, recv_a)), (2, (send_c, recv_c))):
            outbox[turn] = own[index].astype(BF16)
            members, peer = groups[index]

            def post(step):
                send(
                    outbox.at[turn],
                    inbox.at[turn, step - 1],
                    part_send.at[turn, index],
                    part_recv.at[turn, index],
                    peer(step),
                )

            each(members, post)
        return own

    def collect(turn, index, own, inbox):
        await_bytes(inbox.at[turn], part_recv.at[turn, index])
        members = inbox.shape[1]
        if members <= UNROLL:
            result = own
            for step in range(members):
                result = result + inbox[turn, step].astype(F32)
            return result
        return lax.fori_loop(0, members, lambda step, acc: acc + inbox[turn, step].astype(F32), own)

    def share_scalars(turn, values):
        lane = lax.broadcasted_iota(jnp.int32, (1, 128), 1)
        row = jnp.zeros((1, 128), F32)
        for index, value in enumerate(values):
            row = jnp.where(lane == index, value, row)
        send_s[turn] = row

        def post(step):
            send(
                send_s.at[turn],
                recv_s.at[turn, step - 1],
                scal_send.at[turn],
                scal_recv.at[turn],
                peer_all(step),
            )

        each(count, post)
        return row

    def collect_scalars(turn, row, number):
        await_bytes(recv_s.at[turn], scal_recv.at[turn])
        row = row + jnp.sum(recv_s[turn], axis=0)
        return [row[:, index : index + 1] for index in range(number)]

    sums = None
    for chunk in range(chunks):
        span = slice(chunk * rows, (chunk + 1) * rows)
        pairs = (pick(wide_c, chunk) * wide_a[None, :, :]).reshape(rows, columns).astype(BF16)
        paired[span, :] = pairs
        paired_t[:, span] = pairs.T
        values = tensor[chunk * CHUNK_K : (chunk + 1) * CHUNK_K].reshape(rows, width).astype(F32)
        errors = (weight_of(chunk) * (values - mm(pairs, bt))).astype(BF16)
        sums = spread(errors, chunk, sums)
    own = share(0, sums)
    grad_b[...] = collect(0, 1, own[1], recv_b)
    grad_a[...] = collect(0, 0, own[0], recv_a)
    grad_c[...] = collect(0, 2, own[2], recv_c)

    shares = (1.0 / count_a, 1.0 / count_b, 1.0 / count_c)

    def inner(first, second):
        return sum(total(x * y) * part for x, y, part in zip(first, second, shares))

    def tangent_of(chunk, hat_a, hat_bt, hat_c):
        span = slice(chunk * rows, (chunk + 1) * rows)
        sideways = pick(hat_c, chunk) * wide_a[None, :, :] + pick(wide_c, chunk) * hat_a[None, :, :]
        sideways = sideways.reshape(rows, columns).astype(BF16)
        return mm(paired[span, :], hat_bt) + mm(sideways, bt)

    def rounded(triple):
        return (
            triple[0].astype(BF16).astype(F32),
            triple[1].astype(BF16),
            triple[2].astype(BF16).astype(F32),
        )

    gradient = (grad_a[...], grad_b[...], grad_c[...])
    hats = rounded(gradient)
    sums = None
    curve = jnp.zeros((8, width), F32)
    for chunk in range(chunks):
        tangent = tangent_of(chunk, *hats)
        first_t[chunk * rows : (chunk + 1) * rows, :] = tangent
        weighted = weight_of(chunk) * tangent
        curve = curve + fold(weighted * tangent)
        sums = spread(weighted.astype(BF16), chunk, sums)
    own = share(1, sums)
    row = share_scalars(0, (inner(gradient, gradient), total(curve)))
    gradient = (grad_a[...], grad_b[...], grad_c[...])
    product_b = collect(1, 1, own[1], recv_b) + DAMP * gradient[1]
    product_a = collect(1, 0, own[0], recv_a) + DAMP * gradient[0]
    product_c = collect(1, 2, own[2], recv_c) + DAMP * gradient[2]
    norm, curve_first = collect_scalars(0, row, 2)
    step_first = norm / (curve_first + DAMP * norm)
    residual = (
        gradient[0] - step_first * product_a,
        gradient[1] - step_first * product_b,
        gradient[2] - step_first * product_c,
    )

    hats = rounded(residual)
    curve = jnp.zeros((8, width), F32)
    cross = jnp.zeros((8, width), F32)
    for chunk in range(chunks):
        tangent = tangent_of(chunk, *hats)
        weighted = weight_of(chunk) * tangent
        curve = curve + fold(weighted * tangent)
        cross = cross + fold(weighted * first_t[chunk * rows : (chunk + 1) * rows, :])
    row = share_scalars(
        1, (inner(residual, residual), inner(residual, gradient), total(curve), total(cross))
    )

    def owned(flip, turned, own_rank, width_own):
        flip[...] = turned
        start = own_rank * width_own
        if width_own % 8 == 0:
            start = pl.multiple_of(start, 8)
        return flip[pl.ds(start, width_own), :]

    pieces = []
    for out, flip, own_rank, axis, turn in (
        (out_a, flip_a, rank_a, 0, True),
        (out_b, flip_b, rank_b, 1, False),
        (out_c, flip_c, rank_c, 2, True),
    ):
        width_own = out.shape[0]
        first = gradient[axis].T if turn else gradient[axis]
        second = residual[axis].T if turn else residual[axis]
        pieces.append(
            (out, owned(flip, first, own_rank, width_own), owned(flip, second, own_rank, width_own))
        )
    for sem_index, (like, members) in enumerate(
        ((slot_a, count_a), (slot_b, count_b), (slot_c, count_c))
    ):
        await_bytes(like.at[pl.ds(0, members - 1)], gather_send.at[sem_index])
    for turn in range(2):
        for index, inbox in enumerate((recv_a, recv_b, recv_c)):
            await_bytes(inbox.at[turn], part_send.at[turn, index])
        await_bytes(recv_s.at[turn], scal_send.at[turn])
    norm_next, mixed, curve_next, cross_next = collect_scalars(1, row, 4)
    ratio = norm_next / norm
    bottom = (
        curve_next
        + 2.0 * ratio * cross_next
        + ratio * ratio * curve_first
        + DAMP * (norm_next + 2.0 * ratio * mixed + ratio * ratio * norm)
    )
    step_second = norm_next / bottom
    along = step_first + step_second * ratio
    for out, first, second in pieces:
        out[...] = along * first + step_second * second


def local(tensor, observed, factor_a, factor_b, factor_c):
    sizes = (lax.axis_size("ia"), lax.axis_size("ja"), lax.axis_size("ka"))
    size_i, size_j, size_k = sizes
    count_a, count_b, count_c = size_j * size_k, size_i * size_k, size_i * size_j
    count = size_i * size_j * size_k
    depth, height, width = tensor.shape
    inverse = 32.0 / (width * size_j * depth * size_k)
    (own_a, own_b, own_c) = (factor_a.shape[1], factor_b.shape[1], factor_c.shape[1])
    columns = own_a * count_a
    cells = depth * height
    vmem = pltpu.VMEM
    outs = pl.pallas_call(
        functools.partial(kernel, sizes, inverse),
        out_shape=(
            jax.ShapeDtypeStruct((own_a, height), F32),
            jax.ShapeDtypeStruct((own_b, width), F32),
            jax.ShapeDtypeStruct((own_c, depth), F32),
        ),
        in_specs=[pl.BlockSpec(memory_space=pl.ANY)] * 5,
        out_specs=(pl.BlockSpec(memory_space=pltpu.VMEM),) * 3,
        scratch_shapes=[
            vmem((depth, height, width), tensor.dtype),
            vmem((depth, height, width), observed.dtype),
            vmem((count_a, own_a, height), BF16),
            vmem((count_b, own_b, width), BF16),
            vmem((count_c, own_c, depth), BF16),
            vmem((columns, height), F32),
            vmem((columns, width), F32),
            vmem((columns, depth), F32),
            vmem((cells, columns), BF16),
            vmem((columns, cells), BF16),
            vmem((cells, width), F32),
            vmem((2, height, columns), BF16),
            vmem((2, columns, width), BF16),
            vmem((2, depth, columns), BF16),
            vmem((2, count_a - 1, height, columns), BF16),
            vmem((2, count_b - 1, columns, width), BF16),
            vmem((2, count_c - 1, depth, columns), BF16),
            vmem((height, columns), F32),
            vmem((columns, width), F32),
            vmem((depth, columns), F32),
            vmem((2, 1, 128), F32),
            vmem((2, count - 1, 1, 128), F32),
            pltpu.SemaphoreType.DMA((2,)),
            pltpu.SemaphoreType.DMA((3,)),
            pltpu.SemaphoreType.DMA((3,)),
            pltpu.SemaphoreType.DMA((2, 3)),
            pltpu.SemaphoreType.DMA((2, 3)),
            pltpu.SemaphoreType.DMA((2,)),
            pltpu.SemaphoreType.DMA((2,)),
        ],
        compiler_params=pltpu.CompilerParams(collective_id=0, has_side_effects=True),
    )(tensor, observed, factor_a.T, factor_b.T, factor_c.T)
    return tuple(out.T for out in outs)


def solution(mesh):
    placed = (
        P("ka", "ia", "ja"),
        P("ka", "ia", "ja"),
        P("ia", ("ja", "ka")),
        P("ja", ("ia", "ka")),
        P("ka", ("ia", "ja")),
    )
    return jax.shard_map(
        local,
        mesh=mesh,
        in_specs=placed,
        out_specs=(P("ia", ("ja", "ka")), P("ja", ("ia", "ka")), P("ka", ("ia", "ja"))),
        check_vma=False,
    )
```

time: 520 us -> 46 us (0.09)
  blocking collectives: 431 us -> 0 us
  Pallas kernels: 0 us -> 42.4 us
  waiting for transfers between devices: 42.2 us -> 0 us
  between operations: 25.8 us -> 0.65 us
  other arithmetic: 9.88 us -> 0 us
  matrix products: 6.15 us -> 0 us
    psum x9 -> x0, blocking collectives: 364 us -> none  [the longest x3 175 us: settle(): total_c = lax.psum(parts[2], ('ia', 'ja'))]
    all_gather x3 -> x0, blocking collectives: 66.9 us -> none  [the longest x1 30.6 us: local(): full_b = lax.all_gather(factor_b, ('ia', 'ka'), axis=1, tiled=True)]
    pallas_call x0 -> x1, Pallas kernels: none -> 42.4 us  [local(): pl.pallas_call(functools.partial(kernel, sizes, inverse), out_shape=(jax....]
    psum x3 -> x0, waiting for transfers between devices: 42.1 us -> none  [settle(): total_b = lax.psum(parts[1], ('ia', 'ka'))]
    reduce_sum x9 -> x0, other arithmetic: 7.33 us -> none  [inner_sum(): jnp.sum(left_side * right_side) * factor]
    dot_general x11 -> x0, matrix products: 6.15 us -> none  [the longest x3 2.88 us: partials(): lax.dot_general(weighted, paired, (((0,), (0,)), ((), ())), preferred_ele...]
  transfers between devices with their start and end apart: 3 -> 0, of which waited for: 1 -> 0; matrix products, arithmetic and copies ran while one was open for 1% -> 0% of each run, Pallas kernels for 0% -> 0%
where the time goes in v1:
time: 46 us; the launch traced here: 45.7 us
  Pallas kernels  42.4 us (92%)
  local copies, waits for them, and re-layouts  2.67 us (6%)
  between operations  0.65 us (1%)
    pallas_call x1, Pallas kernels, local(): pl.pallas_call(functools.partial(kernel, sizes, inverse), out_shape=(jax....  42.4 us
    unnamed x9, local copies, waits for them, and re-layouts  2.67 us

profile of v1, /device:TPU:0, one launch (start us, length us, event | category | flops | bytes accessed | tf_op | source)
XLA Modules:
  0.0 45.7 jit_solution(1335158380533994597)
XLA Ops:
  0.6 42.4 %shard_map.76 = (f32[16,64]{1,0:T(8,128)}, f32[16,128]{1,0:T(8,128)}, f32[8,32]{1,0:T(8,128)}) custom-call(bf16[32,64,128]{2,1,0:T(8,128)(2,1)} %tensor_hbm.1, s32[32,64,128]{2,1,0:T(8,128)} %observed_hbm.1, bf16[16,64]{1,0:T(8,128)(2,1)} %bitcast.8, bf16[16,128]{1,0:T(8,128)(2,1)} %bitcast.9, bf16[8,32]{1,0:T(8,128)(2,1)} %bitcast.11), custom_call_target="tpu_custom_call" | custom-call | tf_op jit(solution)/shard_map/pallas_call | solution.py:352
  43.0 0.0 copy-start.1
  43.1 0.7 %copy-done.1 = f32[16,64]{1,0:T(8,128)S(1)} copy-done((f32[16,64]{1,0:T(8,128)S(1)}, f32[16,64]{1,0:T(8,128)}, u32[]{:S(2)}) %copy-start.1) | copy-done | bytes 4120
  43.7 0.0 copy-start
  43.7 0.6 %copy.11 = f32[64,16]{0,1:T(8,128)} copy(f32[64,16]{0,1:T(8,128)S(1)} %bitcast.7) | data formatting | bytes 8192
  44.3 0.1 copy-done
  44.4 0.0 copy-start.2
  44.4 0.6 %copy.12 = f32[128,16]{0,1:T(8,128)} copy(f32[128,16]{0,1:T(8,128)S(1)} %bitcast.6) | data formatting | bytes 16384
  45.0 0.1 copy-done.2
  45.1 0.6 %copy.13 = f32[32,8]{0,1:T(8,128)} copy(f32[32,8]{0,1:T(8,128)S(1)} %bitcast.10) | data formatting | bytes 2048
Async XLA Ops:
  43.0 0.7 %copy-start.1 = (f32[16,64]{1,0:T(8,128)S(1)}, f32[16,64]{1,0:T(8,128)}, u32[]{:S(2)}) copy-start(f32[16,64]{1,0:T(8,128)} %get-tuple-element.6) | copy-start | bytes 12292
  43.7 0.7 %copy-start = (f32[16,128]{1,0:T(8,128)S(1)}, f32[16,128]{1,0:T(8,128)}, u32[]{:S(2)}) copy-start(f32[16,128]{1,0:T(8,128)} %get-tuple-element.7) | copy-start | bytes 24580
  44.4 0.7 %copy-start.2 = (f32[8,32]{1,0:T(8,128)S(1)}, f32[8,32]{1,0:T(8,128)}, u32[]{:S(2)}) copy-start(f32[8,32]{1,0:T(8,128)} %get-tuple-element.8) | copy-start | bytes 3076

commit v2 on v1

--- a/solution.py
+++ b/solution.py
@@ -10,6 +10,7 @@
 DAMP = 1.0
 CHUNK_K = 8
 UNROLL = 40
+VMEM_LIMIT = 16 * 2**20
 F32 = jnp.float32
 BF16 = jnp.bfloat16
 
@@ -55,11 +56,15 @@
     paired_t,
     first_t,
     send_a,
-    send_b,
-    send_c,
+    near_out_b,
+    near_out_c,
+    far_out_b,
+    far_out_c,
     recv_a,
-    recv_b,
-    recv_c,
+    near_b,
+    near_c,
+    far_b,
+    far_c,
     grad_a,
     grad_b,
     grad_c,
@@ -97,6 +102,15 @@
         pair = lax.div(other, size_k)
         return (lax.div(pair, size_j), lax.rem(pair, size_j), lax.rem(other, size_k))
 
+    def peer_i(step):
+        return (lax.rem(ia + step, size_i), ja, ka)
+
+    def peer_j(step):
+        return (ia, lax.rem(ja + step, size_j), ka)
+
+    def peer_k(step):
+        return (ia, ja, lax.rem(ka + step, size_k))
+
     groups = ((count_a, peer_a), (count_b, peer_b), (count_c, peer_c))
 
     def send(source, target, send_sem, recv_sem, peer):
@@ -115,33 +129,42 @@
     load_tensor = pltpu.make_async_copy(tensor_hbm, tensor, load_sem.at[0])
     load_observed = pltpu.make_async_copy(observed_hbm, observed, load_sem.at[1])
     shards = ((fa_hbm, slot_a, rank_a), (fb_hbm, slot_b, rank_b), (fc_hbm, slot_c, rank_c))
-    for index, (shard, slots, own) in enumerate(shards):
-        pltpu.make_async_copy(shard, slots.at[own], gather_recv.at[index]).start()
+    own_loads = [
+        pltpu.make_async_copy(shard, slots.at[own], load_sem.at[2 + index])
+        for index, (shard, slots, own) in enumerate(shards)
+    ]
+    for load in own_loads:
+        load.start()
     load_tensor.start()
     load_observed.start()
 
     barrier = pltpu.get_barrier_semaphore()
 
-    def greet(step):
-        pl.semaphore_signal(
-            barrier, inc=1, device_id=peer_all(step), device_id_type=pl.DeviceIdType.MESH
-        )
-
-    each(count, greet)
-    pl.semaphore_wait(barrier, count - 1)
+    def greet(peer):
+        pl.semaphore_signal(barrier, inc=1, device_id=peer, device_id_type=pl.DeviceIdType.MESH)
+
+    for step_i in range(1, size_i):
+        for step_j in range(1, size_j):
+            greet((lax.rem(ia + step_i, size_i), lax.rem(ja + step_j, size_j), ka))
+        for step_k in range(size_k):
+            greet((lax.rem(ia + step_i, size_i), ja, lax.rem(ka + step_k, size_k)))
+    each(count_a, lambda step: greet(peer_a(step)))
+    for load in own_loads:
+        load.wait()
+    pl.semaphore_wait(barrier, (size_i - 1) * (size_j - 1 + size_k) + count_a - 1)
 
     for index in (1, 0, 2):
-        shard, slots, own = shards[index]
+        _, slots, own = shards[index]
         members, peer = groups[index]
 
         def gather(step):
-            send(shard, slots.at[own], gather_send.at[index], gather_recv.at[index], peer(step))
+            send(slots.at[own], slots.at[own], gather_send.at[index], gather_recv.at[index], peer(step))
 
         each(members, gather)
 
     def assemble(index, slots, flip):
-        await_bytes(slots, gather_recv.at[index])
         members, width, _ = slots.shape
+        await_bytes(slots.at[pl.ds(0, members - 1)], gather_recv.at[index])
         for step in range(members):
             flip[step * width : (step + 1) * width, :] = slots[step].astype(F32)
         return flip[...]
@@ -177,33 +200,53 @@
     def fold(array):
         return jnp.sum(array.reshape(rows // 8, 8, width), axis=0)
 
+    hops = (
+        (send_a, recv_a, count_a, peer_a),
+        (near_out_b, near_b, size_k, peer_k),
+        (near_out_c, near_c, size_j, peer_j),
+        (far_out_b, far_b, size_i, peer_i),
+        (far_out_c, far_c, size_i, peer_i),
+    )
+
+    def post(turn, index, value):
+        outbox, inbox, members, peer = hops[index]
+        outbox[turn] = value.astype(BF16)
+
+        def one(step):
+            send(
+                outbox.at[turn],
+                inbox.at[turn, step - 1],
+                part_send.at[turn, index],
+                part_recv.at[turn, index],
+                peer(step),
+            )
+
+        each(members, one)
+
+    def collect(turn, index, own):
+        inbox = hops[index][1]
+        await_bytes(inbox.at[turn], part_recv.at[turn, index])
+        for step in range(inbox.shape[1]):
+            own = own + inbox[turn, step].astype(F32)
+        return own
+
     def share(turn, sums):
-        own = (sums[0], sums[1], jnp.concatenate(sums[2], axis=0))
-        for index, (outbox, inbox) in ((1, (send_b, recv_b)), (0, (send_a, recv_a)), (2, (send_c, recv_c))):
-            outbox[turn] = own[index].astype(BF16)
-            members, peer = groups[index]
-
-            def post(step):
-                send(
-                    outbox.at[turn],
-                    inbox.at[turn, step - 1],
-                    part_send.at[turn, index],
-                    part_recv.at[turn, index],
-                    peer(step),
-                )
-
-            each(members, post)
-        return own
-
-    def collect(turn, index, own, inbox):
-        await_bytes(inbox.at[turn], part_recv.at[turn, index])
-        members = inbox.shape[1]
-        if members <= UNROLL:
-            result = own
-            for step in range(members):
-                result = result + inbox[turn, step].astype(F32)
-            return result
-        return lax.fori_loop(0, members, lambda step, acc: acc + inbox[turn, step].astype(F32), own)
+        sum_a, sum_b, sum_c = sums[0], sums[1], jnp.concatenate(sums[2], axis=0)
+        post(turn, 1, sum_b)
+        post(turn, 2, sum_c)
+        post(turn, 0, sum_a)
+        return sum_a, sum_b, sum_c
+
+    def settle(turn, own):
+        sum_a, sum_b, sum_c = own
+        sum_c = collect(turn, 2, sum_c)
+        post(turn, 4, sum_c)
+        sum_b = collect(turn, 1, sum_b)
+        post(turn, 3, sum_b)
+        sum_a = collect(turn, 0, sum_a)
+        sum_c = collect(turn, 4, sum_c)
+        sum_b = collect(turn, 3, sum_b)
+        return sum_a, sum_b, sum_c
 
     def share_scalars(turn, values):
         lane = lax.broadcasted_iota(jnp.int32, (1, 128), 1)
@@ -239,9 +282,7 @@
         errors = (weight_of(chunk) * (values - mm(pairs, bt))).astype(BF16)
         sums = spread(errors, chunk, sums)
     own = share(0, sums)
-    grad_b[...] = collect(0, 1, own[1], recv_b)
-    grad_a[...] = collect(0, 0, own[0], recv_a)
-    grad_c[...] = collect(0, 2, own[2], recv_c)
+    grad_a[...], grad_b[...], grad_c[...] = settle(0, own)
 
     shares = (1.0 / count_a, 1.0 / count_b, 1.0 / count_c)
 
@@ -274,9 +315,8 @@
     own = share(1, sums)
     row = share_scalars(0, (inner(gradient, gradient), total(curve)))
     gradient = (grad_a[...], grad_b[...], grad_c[...])
-    product_b = collect(1, 1, own[1], recv_b) + DAMP * gradient[1]
-    product_a = collect(1, 0, own[0], recv_a) + DAMP * gradient[0]
-    product_c = collect(1, 2, own[2], recv_c) + DAMP * gradient[2]
+    own = settle(1, own)
+    product_a, product_b, product_c = (part + DAMP * p for part, p in zip(own, gradient))
     norm, curve_first = collect_scalars(0, row, 2)
     step_first = norm / (curve_first + DAMP * norm)
     residual = (
@@ -321,8 +361,8 @@
     ):
         await_bytes(like.at[pl.ds(0, members - 1)], gather_send.at[sem_index])
     for turn in range(2):
-        for index, inbox in enumerate((recv_a, recv_b, recv_c)):
-            await_bytes(inbox.at[turn], part_send.at[turn, index])
+        for index in range(5):
+            await_bytes(hops[index][1].at[turn], part_send.at[turn, index])
         await_bytes(recv_s.at[turn], scal_send.at[turn])
     norm_next, mixed, curve_next, cross_next = collect_scalars(1, row, 4)
     ratio = norm_next / norm
@@ -336,6 +376,17 @@
     along = step_first + step_second * ratio
     for out, first, second in pieces:
         out[...] = along * first + step_second * second
+
+
+def hand_on(in_a, in_b, in_c, out_a, out_b, out_c, sems):
+    copies = [
+        pltpu.make_async_copy(source, target, sems.at[index])
+        for index, (source, target) in enumerate(((in_a, out_a), (in_b, out_b), (in_c, out_c)))
+    ]
+    for copy in copies:
+        copy.start()
+    for copy in copies:
+        copy.wait()
 
 
 def local(tensor, observed, factor_a, factor_b, factor_c):
@@ -349,6 +400,10 @@
     columns = own_a * count_a
     cells = depth * height
     vmem = pltpu.VMEM
+    operands = [
+        pltpu.with_memory_space_constraint(operand, pltpu.HBM)
+        for operand in (tensor, observed, factor_a.T, factor_b.T, factor_c.T)
+    ]
     outs = pl.pallas_call(
         functools.partial(kernel, sizes, inverse),
         out_shape=(
@@ -356,7 +411,7 @@
             jax.ShapeDtypeStruct((own_b, width), F32),
             jax.ShapeDtypeStruct((own_c, depth), F32),
         ),
-        in_specs=[pl.BlockSpec(memory_space=pl.ANY)] * 5,
+        in_specs=[pl.BlockSpec(memory_space=pltpu.HBM)] * 5,
         out_specs=(pl.BlockSpec(memory_space=pltpu.VMEM),) * 3,
         scratch_shapes=[
             vmem((depth, height, width), tensor.dtype),
@@ -373,24 +428,38 @@
             vmem((2, height, columns), BF16),
             vmem((2, columns, width), BF16),
             vmem((2, depth, columns), BF16),
+            vmem((2, columns, width), BF16),
+            vmem((2, depth, columns), BF16),
             vmem((2, count_a - 1, height, columns), BF16),
-            vmem((2, count_b - 1, columns, width), BF16),
-            vmem((2, count_c - 1, depth, columns), BF16),
+            vmem((2, size_k - 1, columns, width), BF16),
+            vmem((2, size_j - 1, depth, columns), BF16),
+            vmem((2, size_i - 1, columns, width), BF16),
+            vmem((2, size_i - 1, depth, columns), BF16),
             vmem((height, columns), F32),
             vmem((columns, width), F32),
             vmem((depth, columns), F32),
             vmem((2, 1, 128), F32),
             vmem((2, count - 1, 1, 128), F32),
-            pltpu.SemaphoreType.DMA((2,)),
+            pltpu.SemaphoreType.DMA((5,)),
             pltpu.SemaphoreType.DMA((3,)),
             pltpu.SemaphoreType.DMA((3,)),
-            pltpu.SemaphoreType.DMA((2, 3)),
-            pltpu.SemaphoreType.DMA((2, 3)),
+            pltpu.SemaphoreType.DMA((2, 5)),
+            pltpu.SemaphoreType.DMA((2, 5)),
             pltpu.SemaphoreType.DMA((2,)),
             pltpu.SemaphoreType.DMA((2,)),
         ],
-        compiler_params=pltpu.CompilerParams(collective_id=0, has_side_effects=True),
-    )(tensor, observed, factor_a.T, factor_b.T, factor_c.T)
+        compiler_params=pltpu.CompilerParams(
+            collective_id=0, has_side_effects=True, vmem_limit_bytes=VMEM_LIMIT
+        ),
+    )(*operands)
+    outs = pl.pallas_call(
+        hand_on,
+        out_shape=tuple(jax.ShapeDtypeStruct(out.shape, F32) for out in outs),
+        in_specs=[pl.BlockSpec(memory_space=pltpu.VMEM)] * 3,
+        out_specs=(pl.BlockSpec(memory_space=pltpu.HBM),) * 3,
+        scratch_shapes=[pltpu.SemaphoreType.DMA((3,))],
+        compiler_params=pltpu.CompilerParams(vmem_limit_bytes=VMEM_LIMIT),
+    )(*outs)
     return tuple(out.T for out in outs)
 
 

time: 46 us -> 37 us (0.80)
  Pallas kernels: 42.4 us -> 36.2 us
  local copies, waits for them, and re-layouts: 2.67 us -> 0 us
    pallas_call x1, Pallas kernels: 42.4 us -> 35.6 us  [local(): pl.pallas_call(functools.partial(kernel, sizes, inverse), out_shape=(jax....]
    unnamed x9 -> x0, local copies, waits for them, and re-layouts: 2.67 us -> none
    pallas_call x0 -> x1, Pallas kernels: none -> 0.63 us  [local(): pl.pallas_call(hand_on, out_shape=tuple((jax.ShapeDtypeStruct(out.shape,...]
where the time goes in v2:
time: 37 us; the launch traced here: 36.8 us
  Pallas kernels  36.2 us (98%)
  between operations  0.64 us (2%)
    pallas_call x1, Pallas kernels, local(): pl.pallas_call(functools.partial(kernel, sizes, inverse), out_shape=(jax....  35.6 us

profile of v2, /device:TPU:0, one launch (start us, length us, event | category | flops | bytes accessed | tf_op | source)
XLA Modules:
  0.0 36.8 jit_solution(8458367637055171990)
XLA Ops:
  0.6 35.6 %shard_map.76 = (f32[16,64]{1,0:T(8,128)S(1)}, f32[16,128]{1,0:T(8,128)S(1)}, f32[8,32]{1,0:T(8,128)S(1)}) custom-call(bf16[32,64,128]{2,1,0:T(8,128)(2,1)} %tensor_hbm.1, s32[32,64,128]{2,1,0:T(8,128)} %observed_hbm.1, bf16[16,64]{1,0:T(8,128)(2,1)} %bitcast.6, bf16[16,128]{1,0:T(8,128)(2,1)} %bitcast.7, bf16[8,32]{1,0:T(8,128)(2,1)} %bitcast.8), custom_call_target="tpu_custom_call" | custom-call | tf_op jit(solution)/shard_map/pallas_call | solution.py:407
  36.2 0.6 %shard_map.77 = (f32[16,64]{1,0:T(8,128)}, f32[16,128]{1,0:T(8,128)}, f32[8,32]{1,0:T(8,128)}) custom-call(f32[16,64]{1,0:T(8,128)S(1)} %get-tuple-element.9.in_a, f32[16,128]{1,0:T(8,128)S(1)} %get-tuple-element.10.in_b, f32[8,32]{1,0:T(8,128)S(1)} %get-tuple-element.11.in_c), custom_call_target="tpu_custom_call" | custom-call | tf_op jit(solution)/shard_map/pallas_call | solution.py:455

commit v3 on v2

--- a/solution.py
+++ b/solution.py
@@ -55,6 +55,7 @@
     paired,
     paired_t,
     first_t,
+    second_t,
     send_a,
     near_out_b,
     near_out_c,
@@ -126,6 +127,17 @@
     def await_bytes(like, sem):
         pltpu.make_async_copy(like, like, sem).wait()
 
+    barrier = pltpu.get_barrier_semaphore()
+
+    def greet(peer):
+        pl.semaphore_signal(barrier, inc=1, device_id=peer, device_id_type=pl.DeviceIdType.MESH)
+
+    for step_i in range(1, size_i):
+        for step_j in range(1, size_j):
+            greet((lax.rem(ia + step_i, size_i), lax.rem(ja + step_j, size_j), ka))
+        for step_k in range(size_k):
+            greet((lax.rem(ia + step_i, size_i), ja, lax.rem(ka + step_k, size_k)))
+    each(count_a, lambda step: greet(peer_a(step)))
     load_tensor = pltpu.make_async_copy(tensor_hbm, tensor, load_sem.at[0])
     load_observed = pltpu.make_async_copy(observed_hbm, observed, load_sem.at[1])
     shards = ((fa_hbm, slot_a, rank_a), (fb_hbm, slot_b, rank_b), (fc_hbm, slot_c, rank_c))
@@ -138,22 +150,11 @@
     load_tensor.start()
     load_observed.start()
 
-    barrier = pltpu.get_barrier_semaphore()
-
-    def greet(peer):
-        pl.semaphore_signal(barrier, inc=1, device_id=peer, device_id_type=pl.DeviceIdType.MESH)
-
-    for step_i in range(1, size_i):
-        for step_j in range(1, size_j):
-            greet((lax.rem(ia + step_i, size_i), lax.rem(ja + step_j, size_j), ka))
-        for step_k in range(size_k):
-            greet((lax.rem(ia + step_i, size_i), ja, lax.rem(ka + step_k, size_k)))
-    each(count_a, lambda step: greet(peer_a(step)))
     for load in own_loads:
         load.wait()
     pl.semaphore_wait(barrier, (size_i - 1) * (size_j - 1 + size_k) + count_a - 1)
 
-    for index in (1, 0, 2):
+    for index in (2, 0, 1):
         _, slots, own = shards[index]
         members, peer = groups[index]
 
@@ -171,15 +172,10 @@
 
     wide_a = assemble(0, slot_a, flip_a).T
     wide_c = assemble(2, slot_c, flip_c).T
-    turned_b = assemble(1, slot_b, flip_b)
-    bt = turned_b.astype(BF16)
-    full_b = turned_b.T.astype(BF16)
     depth, height, width = tensor.shape
     columns = wide_a.shape[1]
     rows = CHUNK_K * height
     chunks = depth // CHUNK_K
-    load_tensor.wait()
-    load_observed.wait()
 
     def weight_of(chunk):
         cells = observed[chunk * CHUNK_K : (chunk + 1) * CHUNK_K].reshape(rows, width)
@@ -187,6 +183,17 @@
 
     def pick(wide, chunk):
         return wide[chunk * CHUNK_K : (chunk + 1) * CHUNK_K][:, None, :]
+
+    for chunk in range(chunks):
+        span = slice(chunk * rows, (chunk + 1) * rows)
+        pairs = (pick(wide_c, chunk) * wide_a[None, :, :]).reshape(rows, columns).astype(BF16)
+        paired[span, :] = pairs
+        paired_t[:, span] = pairs.T
+    turned_b = assemble(1, slot_b, flip_b)
+    bt = turned_b.astype(BF16)
+    full_b = turned_b.T.astype(BF16)
+    load_tensor.wait()
+    load_observed.wait()
 
     def spread(weighted, chunk, sums):
         mixture = mm(weighted, full_b).reshape(CHUNK_K, height, columns)
@@ -234,18 +241,17 @@
         sum_a, sum_b, sum_c = sums[0], sums[1], jnp.concatenate(sums[2], axis=0)
         post(turn, 1, sum_b)
         post(turn, 2, sum_c)
-        post(turn, 0, sum_a)
         return sum_a, sum_b, sum_c
 
-    def settle(turn, own):
+    def settle_ac(turn, own):
         sum_a, sum_b, sum_c = own
         sum_c = collect(turn, 2, sum_c)
         post(turn, 4, sum_c)
         sum_b = collect(turn, 1, sum_b)
         post(turn, 3, sum_b)
+        post(turn, 0, sum_a)
         sum_a = collect(turn, 0, sum_a)
         sum_c = collect(turn, 4, sum_c)
-        sum_b = collect(turn, 3, sum_b)
         return sum_a, sum_b, sum_c
 
     def share_scalars(turn, values):
@@ -275,67 +281,72 @@
     sums = None
     for chunk in range(chunks):
         span = slice(chunk * rows, (chunk + 1) * rows)
-        pairs = (pick(wide_c, chunk) * wide_a[None, :, :]).reshape(rows, columns).astype(BF16)
-        paired[span, :] = pairs
-        paired_t[:, span] = pairs.T
         values = tensor[chunk * CHUNK_K : (chunk + 1) * CHUNK_K].reshape(rows, width).astype(F32)
-        errors = (weight_of(chunk) * (values - mm(pairs, bt))).astype(BF16)
+        errors = (weight_of(chunk) * (values - mm(paired[span, :], bt))).astype(BF16)
         sums = spread(errors, chunk, sums)
     own = share(0, sums)
-    grad_a[...], grad_b[...], grad_c[...] = settle(0, own)
-
     shares = (1.0 / count_a, 1.0 / count_b, 1.0 / count_c)
 
-    def inner(first, second):
-        return sum(total(x * y) * part for x, y, part in zip(first, second, shares))
-
-    def tangent_of(chunk, hat_a, hat_bt, hat_c):
-        span = slice(chunk * rows, (chunk + 1) * rows)
-        sideways = pick(hat_c, chunk) * wide_a[None, :, :] + pick(wide_c, chunk) * hat_a[None, :, :]
-        sideways = sideways.reshape(rows, columns).astype(BF16)
-        return mm(paired[span, :], hat_bt) + mm(sideways, bt)
-
-    def rounded(triple):
-        return (
-            triple[0].astype(BF16).astype(F32),
-            triple[1].astype(BF16),
-            triple[2].astype(BF16).astype(F32),
-        )
-
-    gradient = (grad_a[...], grad_b[...], grad_c[...])
-    hats = rounded(gradient)
+    def inner(first, second, axes):
+        return sum(total(first[axis] * second[axis]) * shares[axis] for axis in axes)
+
+    def span_of(chunk):
+        return slice(chunk * rows, (chunk + 1) * rows)
+
+    def sideways_of(result, hat_a, hat_c):
+        for chunk in range(chunks):
+            mixed_a = pick(hat_c, chunk) * wide_a[None, :, :]
+            mixed_c = pick(wide_c, chunk) * hat_a[None, :, :]
+            result[span_of(chunk), :] = mm((mixed_a + mixed_c).reshape(rows, columns).astype(BF16), bt)
+
+    def wide_hat(array):
+        return array.astype(BF16).astype(F32)
+
+    sum_a, sum_b, sum_c = settle_ac(0, own)
+    grad_a[...] = sum_a
+    grad_c[...] = sum_c
+    sideways_of(first_t, wide_hat(sum_a), wide_hat(sum_c))
+    sum_b = collect(0, 3, sum_b)
+    grad_b[...] = sum_b
+
+    hat_b = sum_b.astype(BF16)
     sums = None
     curve = jnp.zeros((8, width), F32)
     for chunk in range(chunks):
-        tangent = tangent_of(chunk, *hats)
-        first_t[chunk * rows : (chunk + 1) * rows, :] = tangent
+        tangent = first_t[span_of(chunk), :] + mm(paired[span_of(chunk), :], hat_b)
+        first_t[span_of(chunk), :] = tangent
         weighted = weight_of(chunk) * tangent
         curve = curve + fold(weighted * tangent)
         sums = spread(weighted.astype(BF16), chunk, sums)
     own = share(1, sums)
-    row = share_scalars(0, (inner(gradient, gradient), total(curve)))
     gradient = (grad_a[...], grad_b[...], grad_c[...])
-    own = settle(1, own)
-    product_a, product_b, product_c = (part + DAMP * p for part, p in zip(own, gradient))
+    row = share_scalars(0, (inner(gradient, gradient, (0, 1, 2)), total(curve)))
+    sum_a, sum_b, sum_c = settle_ac(1, own)
     norm, curve_first = collect_scalars(0, row, 2)
     step_first = norm / (curve_first + DAMP * norm)
-    residual = (
-        gradient[0] - step_first * product_a,
-        gradient[1] - step_first * product_b,
-        gradient[2] - step_first * product_c,
-    )
-
-    hats = rounded(residual)
+    gradient = (grad_a[...], grad_b[...], grad_c[...])
+
+    def residual_of(axis, part):
+        return gradient[axis] - step_first * (part + DAMP * gradient[axis])
+
+    rest_a, rest_c = residual_of(0, sum_a), residual_of(2, sum_c)
+    sideways_of(second_t, wide_hat(rest_a), wide_hat(rest_c))
+    residual = (rest_a, None, rest_c)
+    norm_next = inner(residual, residual, (0, 2))
+    mixed = inner(residual, gradient, (0, 2))
+    residual = (rest_a, residual_of(1, collect(1, 3, sum_b)), rest_c)
+
+    hat_b = residual[1].astype(BF16)
     curve = jnp.zeros((8, width), F32)
     cross = jnp.zeros((8, width), F32)
     for chunk in range(chunks):
-        tangent = tangent_of(chunk, *hats)
+        tangent = second_t[span_of(chunk), :] + mm(paired[span_of(chunk), :], hat_b)
         weighted = weight_of(chunk) * tangent
         curve = curve + fold(weighted * tangent)
-        cross = cross + fold(weighted * first_t[chunk * rows : (chunk + 1) * rows, :])
-    row = share_scalars(
-        1, (inner(residual, residual), inner(residual, gradient), total(curve), total(cross))
-    )
+        cross = cross + fold(weighted * first_t[span_of(chunk), :])
+    norm_next = norm_next + inner(residual, residual, (1,))
+    mixed = mixed + inner(residual, gradient, (1,))
+    row = share_scalars(1, (norm_next, mixed, total(curve), total(cross)))
 
     def owned(flip, turned, own_rank, width_own):
         flip[...] = turned
@@ -424,6 +435,7 @@
             vmem((columns, depth), F32),
             vmem((cells, columns), BF16),
             vmem((columns, cells), BF16),
+            vmem((cells, width), F32),
             vmem((cells, width), F32),
             vmem((2, height, columns), BF16),
             vmem((2, columns, width), BF16),

time: 37 us -> 36.3 us (0.981)
  Pallas kernels: 36.2 us -> 35.5 us
    pallas_call x1, Pallas kernels: 35.6 us -> 34.8 us  [local(): pl.pallas_call(functools.partial(kernel, sizes, inverse), out_shape=(jax....]
where the time goes in v3:
time: 36.3 us; the launch traced here: 36.1 us
  Pallas kernels  35.5 us (98%)
  between operations  0.64 us (2%)
    pallas_call x1, Pallas kernels, local(): pl.pallas_call(functools.partial(kernel, sizes, inverse), out_shape=(jax....  34.8 us

profile of v3, /device:TPU:0, one launch (start us, length us, event | category | flops | bytes accessed | tf_op | source)
XLA Modules:
  0.0 36.1 jit_solution(1550335129082312166)
XLA Ops:
  0.6 34.8 %shard_map.76 = (f32[16,64]{1,0:T(8,128)S(1)}, f32[16,128]{1,0:T(8,128)S(1)}, f32[8,32]{1,0:T(8,128)S(1)}) custom-call(bf16[32,64,128]{2,1,0:T(8,128)(2,1)} %tensor_hbm.1, s32[32,64,128]{2,1,0:T(8,128)} %observed_hbm.1, bf16[16,64]{1,0:T(8,128)(2,1)} %bitcast.6, bf16[16,128]{1,0:T(8,128)(2,1)} %bitcast.7, bf16[8,32]{1,0:T(8,128)(2,1)} %bitcast.8), custom_call_target="tpu_custom_call" | custom-call | tf_op jit(solution)/shard_map/pallas_call | solution.py:418
  35.5 0.6 %shard_map.77 = (f32[16,64]{1,0:T(8,128)}, f32[16,128]{1,0:T(8,128)}, f32[8,32]{1,0:T(8,128)}) custom-call(f32[16,64]{1,0:T(8,128)S(1)} %get-tuple-element.9.in_a, f32[16,128]{1,0:T(8,128)S(1)} %get-tuple-element.10.in_b, f32[8,32]{1,0:T(8,128)S(1)} %get-tuple-element.11.in_c), custom_call_target="tpu_custom_call" | custom-call | tf_op jit(solution)/shard_map/pallas_call | solution.py:467

commit v4 on v3

--- a/solution.py
+++ b/solution.py
@@ -112,6 +112,13 @@
     def peer_k(step):
         return (ia, ja, lax.rem(ka + step, size_k))
 
+    low = ia * 2 < size_i
+    mirrored = jnp.where(low, size_i - 1 - ia, ia)
+
+    def distant(turn):
+        spot = turn + jnp.where(turn >= mirrored, 1, 0)
+        return jnp.where(low, size_i - 1 - spot, spot)
+
     groups = ((count_a, peer_a), (count_b, peer_b), (count_c, peer_c))
 
     def send(source, target, send_sem, recv_sem, peer):
@@ -218,6 +225,17 @@
     def post(turn, index, value):
         outbox, inbox, members, peer = hops[index]
         outbox[turn] = value.astype(BF16)
+        if index >= 3:
+            for order in range(size_i - 1):
+                target = distant(order)
+                send(
+                    outbox.at[turn],
+                    inbox.at[turn, lax.rem(target - ia + size_i, size_i) - 1],
+                    part_send.at[turn, index],
+                    part_recv.at[turn, index],
+                    (target, ja, ka),
+                )
+            return
 
         def one(step):
             send(

time: 36.3 us -> 35.9 us (0.989)
  Pallas kernels: 35.5 us -> 35.1 us
where the time goes in v4:
time: 35.9 us; the launch traced here: 35.8 us
  Pallas kernels  35.1 us (98%)
  between operations  0.64 us (2%)
    pallas_call x1, Pallas kernels, local(): pl.pallas_call(functools.partial(kernel, sizes, inverse), out_shape=(jax....  34.5 us

profile of v4, /device:TPU:0, one launch (start us, length us, event | category | flops | bytes accessed | tf_op | source)
XLA Modules:
  0.0 35.8 jit_solution(12029375991136605523)
XLA Ops:
  0.6 34.5 %shard_map.76 = (f32[16,64]{1,0:T(8,128)S(1)}, f32[16,128]{1,0:T(8,128)S(1)}, f32[8,32]{1,0:T(8,128)S(1)}) custom-call(bf16[32,64,128]{2,1,0:T(8,128)(2,1)} %tensor_hbm.1, s32[32,64,128]{2,1,0:T(8,128)} %observed_hbm.1, bf16[16,64]{1,0:T(8,128)(2,1)} %bitcast.6, bf16[16,128]{1,0:T(8,128)(2,1)} %bitcast.7, bf16[8,32]{1,0:T(8,128)(2,1)} %bitcast.8), custom_call_target="tpu_custom_call" | custom-call | tf_op jit(solution)/shard_map/pallas_call | solution.py:436
  35.1 0.6 %shard_map.77 = (f32[16,64]{1,0:T(8,128)}, f32[16,128]{1,0:T(8,128)}, f32[8,32]{1,0:T(8,128)}) custom-call(f32[16,64]{1,0:T(8,128)S(1)} %get-tuple-element.9.in_a, f32[16,128]{1,0:T(8,128)S(1)} %get-tuple-element.10.in_b, f32[8,32]{1,0:T(8,128)S(1)} %get-tuple-element.11.in_c), custom_call_target="tpu_custom_call" | custom-call | tf_op jit(solution)/shard_map/pallas_call | solution.py:485
